TPU v7x, 256 devices: a whole 4x4x8 slice. The times are simulated.
256 devices in a mesh: feat: 16 (over z, core), dom: 16 (over x, y).
Axes of the slice: x: 4, y: 4, z: 8, core: 2. Of those that a mesh axis runs over, the one named last changes fastest.
Arguments:
- features: bfloat16 [16, 1024, 9216], P('dom', 'feat'), may hold values from -6 to 6
- w1_self: bfloat16 [1024, 256], P('feat'), may hold values from -0.1875 to 0.1875
- w1_neigh: bfloat16 [1024, 256], P('feat'), may hold values from -0.1875 to 0.1875
- w2_self: bfloat16 [256, 256], replicated, may hold values from -0.375 to 0.375
- w2_neigh: bfloat16 [256, 256], replicated, may hold values from -0.375 to 0.375
- neigh_one: int32 [16, 10, 4608], P('dom'), may hold values from 0 to 9215
- send_rows: int32 [16, 16, 16, 128], P('dom', 'feat'), may hold values from 0 to 287
- recv_count: int32 [16, 16, 16], P(None, 'feat', 'dom'), may hold values from 1 to 128, as said below
- neigh_two: int32 [16, 16, 256, 15], P('dom', 'feat'), may hold values from 0 to 2047, as said below
- seed_rows: int32 [16, 16, 256], P('dom', 'feat'), may hold values from 0 to 287, as said below
- d_out: bfloat16 [16, 16, 256, 256], P('dom', 'feat'), may hold values from -0.0625 to 0.0625
Outputs:
- layer_two: bfloat16 [16, 16, 256, 256], P('dom', 'feat')
- grad_w1_self: float32 [1024, 256], P('feat')
- grad_w1_neigh: float32 [1024, 256], P('feat')
- grad_w2_self: float32 [256, 256], replicated
- grad_w2_neigh: float32 [256, 256], replicated
Inputs may be any that keep to these rules, and one draw needn't show every extreme that they name: `neigh_one`: columns of the partition's 9216 input nodes. `send_rows`: rows among the sending device's 288 owned nodes. `recv_count`: the live slots of a buffer are its leading ones; every receiver gets a full buffer of 128 live rows from some source, and some receiver gets full buffers from every source. `neigh_two`: each is below the total of the receiving device's counts; on every device some seed names the last live row. `seed_rows`: distinct within one device.
All inputs are finite; a program needn't handle non-finite values.
Results may differ from a plain program's by a relative error of at most 0.0051.
Values may be sent and summed in bfloat16 or wider, within the bound.
No kernel may reach another device: no remote copies, remote signals or barrier semaphores. Data moves between devices by JAX's collectives and lax.ppermute only.
A program may use at most 64 MiB of HBM per device.

v0:
```python
import jax
import jax.numpy as jnp
from jax import lax
from jax.sharding import PartitionSpec as P


def rows_of(source_table, index_rows):
    return jnp.take(source_table, index_rows, axis=0)


def contract_rows(left_side, right_side):
    return lax.dot_general(
        left_side, right_side, (((0,), (0,)), ((), ())), preferred_element_type=jnp.float32
    )


def contract_cols(left_side, right_side):
    return lax.dot_general(
        left_side, right_side, (((1,), (1,)), ((), ())), preferred_element_type=jnp.float32
    )


def per_device(
    features,
    w1_self,
    w1_neigh,
    w2_self,
    w2_neigh,
    neigh_one,
    send_rows,
    recv_count,
    neigh_two,
    seed_rows,
    d_out,
):
    feature_table = features[0]
    neigh_lists = neigh_one[0]
    target_rows = neigh_lists.shape[1]
    fan_one = neigh_lists.shape[0]
    running = jnp.zeros((feature_table.shape[0], target_rows), jnp.float32)
    for column in range(fan_one):
        running = running + jnp.take(feature_table, neigh_lists[column], axis=1).astype(jnp.float32)
    mean_one = (running / fan_one).astype(jnp.bfloat16)
    own_self = feature_table[:, :target_rows]
    owned_rows = target_rows // lax.axis_size("feat")
    hidden_width = w1_self.shape[1]
    left_self = own_self
    left_mean = mean_one
    pre_one = lax.psum_scatter(
        contract_rows(left_self, w1_self) + contract_rows(left_mean, w1_neigh),
        "feat",
        scatter_dimension=0,
        tiled=True,
    )
    hidden = jax.nn.elu(pre_one).astype(jnp.bfloat16)
    send_index = send_rows[0, 0]
    peer_count = send_index.shape[0]
    slot_count = send_index.shape[1]
    outgoing = rows_of(hidden, send_index.reshape(-1)).reshape(peer_count, slot_count, hidden_width)
    incoming = lax.all_to_all(outgoing, "dom", split_axis=0, concat_axis=0, tiled=True)
    flat_in = incoming.reshape(peer_count * slot_count, hidden_width)
    counts = recv_count[:, 0, 0]
    starts = jnp.cumsum(counts) - counts
    positions = neigh_two[0, 0]
    source = jnp.sum((positions[:, :, None] >= starts[None, None, 1:]).astype(jnp.int32), axis=2)
    picked = (source[:, :, None] == jnp.arange(peer_count, dtype=jnp.int32)).astype(jnp.int32)
    offset_of = jnp.sum(picked * starts[None, None, :], axis=2)
    where_in = source * slot_count + positions - offset_of
    fan_two = positions.shape[1]
    seed_count = positions.shape[0]
    running_two = jnp.zeros((seed_count, hidden_width), jnp.float32)
    for column in range(fan_two):
        running_two = running_two + rows_of(flat_in, where_in[:, column]).astype(jnp.float32)
    mean_two = (running_two / fan_two).astype(jnp.bfloat16)
    seeds = seed_rows[0, 0]
    self_two = rows_of(hidden, seeds)
    grad_out = d_out[0, 0]
    layer_out = (
        jnp.dot(self_two, w2_self, preferred_element_type=jnp.float32)
        + jnp.dot(mean_two, w2_neigh, preferred_element_type=jnp.float32)
    ).astype(jnp.bfloat16)
    local_w2_self = contract_rows(self_two, grad_out)
    local_w2_neigh = contract_rows(mean_two, grad_out)
    d_self = contract_cols(grad_out, w2_self)
    d_mean = contract_cols(grad_out, w2_neigh) / fan_two
    slot_sum = jnp.zeros((peer_count * slot_count, hidden_width), jnp.float32)
    for column in range(fan_two):
        slot_sum = slot_sum.at[where_in[:, column]].add(d_mean)
    slot_grad = slot_sum.astype(jnp.bfloat16).reshape(peer_count, slot_count, hidden_width)
    returned = lax.all_to_all(slot_grad, "dom", split_axis=0, concat_axis=0, tiled=True)
    d_hidden = jnp.zeros((owned_rows, hidden_width), jnp.float32)
    d_hidden = d_hidden.at[send_index.reshape(-1)].add(
        returned.reshape(-1, hidden_width).astype(jnp.float32)
    )
    d_hidden = d_hidden.at[seeds].add(d_self)
    elu_slope = jnp.where(pre_one > 0, 1.0, jnp.exp(jnp.minimum(pre_one, 0.0)))
    d_pre = (d_hidden * elu_slope).astype(jnp.bfloat16)
    piece = lax.all_gather(d_pre, "feat", axis=0, tiled=True)
    left_self = own_self
    left_mean = mean_one
    first_self = jnp.dot(left_self, piece, preferred_element_type=jnp.float32)
    first_mean = jnp.dot(left_mean, piece, preferred_element_type=jnp.float32)
    first_self, first_mean = lax.psum((first_self, first_mean), "dom")
    second_self, second_mean = lax.psum((local_w2_self, local_w2_neigh), ("feat", "dom"))
    return (layer_out[None, None], first_self, first_mean, second_self, second_mean)


def solution(mesh):
    return jax.shard_map(
        per_device,
        mesh=mesh,
        in_specs=(
            P("dom", "feat", None),
            P("feat", None),
            P("feat", None),
            P(),
            P(),
            P("dom", None, None),
            P("dom", "feat", None, None),
            P(None, "feat", "dom"),
            P("dom", "feat", None, None),
            P("dom", "feat", None),
            P("dom", "feat", None, None),
        ),
        out_specs=(P("dom", "feat", None, None), P("feat", None), P("feat", None), P(), P()),
        check_vma=False,
    )
```

profile of v0, /device:TPU:2, one launch (start us, length us, event | category | flops | bytes accessed | tf_op | source)
XLA Modules:
  0.0 690.3 jit_solution(7600817708877585368)
XLA Ops:
  7.2 1.2 slice_reduce_fusion.9
  8.7 2.8 copy.24
  11.5 10.1 %gather_fusion.2 = bf16[4608,64]{1,0:T(8,128)(2,1)} fusion(bf16[64,9216]{0,1:T(8,128)(2,1)S(1)} %bitcast.99, s32[5120]{0:T(1024)S(1)} %pad_clamp_fusion.9), kind=kCustom, calls=%fused_computation.clone | custom fusion | bytes 1198080 | tf_op jit(solution)/shard_map/jit(_take)/gather | solution.py:42
  21.6 10.1 %gather_fusion.3 = bf16[4608,64]{1,0:T(8,128)(2,1)} fusion(bf16[64,9216]{0,1:T(8,128)(2,1)S(1)} %bitcast.100, s32[5120]{0:T(1024)S(1)} %pad_clamp_fusion.8), kind=kCustom, calls=%fused_computation.2.clone | custom fusion | bytes 1198080 | tf_op jit(solution)/shard_map/jit(_take)/gather | solution.py:42
  31.7 10.1 %gather_fusion.4 = bf16[4608,64]{1,0:T(8,128)(2,1)} fusion(bf16[64,9216]{0,1:T(8,128)(2,1)S(1)} %bitcast.101, s32[5120]{0:T(1024)S(1)} %pad_clamp_fusion.7), kind=kCustom, calls=%fused_computation.3.clone | custom fusion | bytes 1198080 | tf_op jit(solution)/shard_map/jit(_take)/gather | solution.py:42
  41.8 10.1 %gather_fusion.5 = bf16[4608,64]{1,0:T(8,128)(2,1)} fusion(bf16[64,9216]{0,1:T(8,128)(2,1)S(1)} %bitcast.102, s32[5120]{0:T(1024)S(1)} %pad_clamp_fusion.6), kind=kCustom, calls=%fused_computation.4.clone | custom fusion | bytes 1198080 | tf_op jit(solution)/shard_map/jit(_take)/gather | solution.py:42
  51.9 10.1 %gather_fusion.6 = bf16[4608,64]{1,0:T(8,128)(2,1)} fusion(bf16[64,9216]{0,1:T(8,128)(2,1)S(1)} %bitcast.103, s32[5120]{0:T(1024)S(1)} %pad_clamp_fusion.5), kind=kCustom, calls=%fused_computation.5.clone | custom fusion | bytes 1198080 | tf_op jit(solution)/shard_map/jit(_take)/gather | solution.py:42
  62.1 10.1 %gather_fusion.7 = bf16[4608,64]{1,0:T(8,128)(2,1)} fusion(bf16[64,9216]{0,1:T(8,128)(2,1)S(1)} %bitcast.104, s32[5120]{0:T(1024)S(1)} %pad_clamp_fusion.4), kind=kCustom, calls=%fused_computation.6.clone | custom fusion | bytes 1198080 | tf_op jit(solution)/shard_map/jit(_take)/gather | solution.py:42
  72.2 10.1 %gather_fusion.8 = bf16[4608,64]{1,0:T(8,128)(2,1)} fusion(bf16[64,9216]{0,1:T(8,128)(2,1)S(1)} %bitcast.105, s32[5120]{0:T(1024)S(1)} %pad_clamp_fusion.3), kind=kCustom, calls=%fused_computation.7.clone | custom fusion | bytes 1198080 | tf_op jit(solution)/shard_map/jit(_take)/gather | solution.py:42
  82.3 10.1 %gather_fusion.9 = bf16[4608,64]{1,0:T(8,128)(2,1)} fusion(bf16[64,9216]{0,1:T(8,128)(2,1)S(1)} %bitcast.106, s32[5120]{0:T(1024)S(1)} %pad_clamp_fusion.2), kind=kCustom, calls=%fused_computation.8.clone | custom fusion | bytes 1198080 | tf_op jit(solution)/shard_map/jit(_take)/gather | solution.py:42
  92.4 10.1 %gather_fusion.10 = bf16[4608,64]{1,0:T(8,128)(2,1)} fusion(bf16[64,9216]{0,1:T(8,128)(2,1)S(1)} %bitcast.107, s32[5120]{0:T(1024)S(1)} %pad_clamp_fusion.1), kind=kCustom, calls=%fused_computation.9.clone | custom fusion | bytes 1198080 | tf_op jit(solution)/shard_map/jit(_take)/gather | solution.py:42
  102.6 10.1 %gather_fusion.11 = bf16[4608,64]{1,0:T(8,128)(2,1)} fusion(bf16[64,9216]{0,1:T(8,128)(2,1)S(1)} %bitcast.108, s32[5120]{0:T(1024)S(1)} %pad_clamp_fusion), kind=kCustom, calls=%fused_computation.10.clone | custom fusion | bytes 1198080 | tf_op jit(solution)/shard_map/jit(_take)/gather | solution.py:42
  116.8 10.3 %multiply_convert_fusion = bf16[64,4608]{0,1:T(8,128)(2,1)S(1)} fusion(bf16[4608,64]{1,0:T(8,128)(2,1)} %gather_fusion.11, bf16[4608,64]{1,0:T(8,128)(2,1)S(1)} %copy-done.11, bf16[4608,64]{1,0:T(8,128)(2,1)S(1)} %copy-done.10, bf16[4608,64]{1,0:T(8,128)(2,1)S(1)} %copy-done.9, bf16[4608,64]{1,0:T(8,128)(2,1)S(1)} %copy-done.8, ...), kind=kLoop, calls=%fused_computation.45 | loop fusion | flops 9142272 | bytes 6534144 | tf_op jit(solution)/shard_map/convert_element_type | solution.py:43
  128.1 2.9 convolution_add_fusion
  133.0 3.4 scatter_custom_fusion
  136.4 4.7 scatter_fusion
  141.2 5.2 scatter_fusion.1
  146.3 4.7 scatter_fusion.2
  151.1 4.8 scatter_fusion.3
  155.8 4.7 scatter_fusion.4
  160.6 4.7 scatter_fusion.5
  165.3 4.8 scatter_fusion.6
  170.1 4.8 scatter_fusion.7
  174.8 4.7 scatter_fusion.8
  179.5 4.8 scatter_fusion.9
  184.3 4.8 scatter_fusion.10
  189.1 4.9 scatter_fusion.11
  194.0 4.7 scatter_fusion.12
  198.7 4.7 scatter_fusion.13
  203.4 2.8 convert_element_type.133
  206.2 7.5 %all-to-all-start.1 = ((bf16[16,128,256]{2,1,0:T(8,128)(2,1)}), bf16[16,128,256]{2,1,0:T(8,128)(2,1)S(1)}, u32[]{:S(2)}, u32[]{:S(2)}) async-start(bf16[16,128,256]{2,1,0:T(8,128)(2,1)} %bitcast.53), calls=%async_computation.2 | async-start | bytes 2097152 | tf_op jit(solution)/shard_map/all_to_all | solution.py:90
  225.6 1.8 fusion.18
  229.7 11.0 %scatter_custom_fusion.15 = f32[288,256]{1,0:T(8,128)S(1)} fusion(s32[2048]{0:T(1024)S(1)} %bitcast.115, bf16[2048,256]{1,0:T(8,128)(2,1)} %bitcast.111, f32[]{:T(128)} %constant.47.clone.1), kind=kCustom, calls=%fused_computation.46 | custom fusion | flops 1048576 | bytes 1343492 | tf_op jit(solution)/shard_map/scatter-add | solution.py:92
  240.9 2.5 scatter_fusion.14
  243.4 1.8 fusion.12
  249.9 9.0 %gather_fusion.1 = bf16[2048,256]{1,0:T(8,128)(2,1)} fusion(bf16[288,256]{1,0:T(8,128)(2,1)S(1)} %get-tuple-element.22, s32[2048]{0:T(1024)S(1)} %broadcast_clamp_fusion), kind=kCustom, calls=%fused_computation.26 | custom fusion | bytes 2105344 | tf_op jit(solution)/shard_map/jit(_take)/gather | solution.py:8
  258.9 2.3 broadcast_select_fusion
  261.2 7.0 %all-to-all-start = ((bf16[16,128,256]{2,1,0:T(8,128)(2,1)}), bf16[16,128,256]{2,1,0:T(8,128)(2,1)}, u32[]{:S(2)}, u32[]{:S(2)}) async-start(bf16[16,128,256]{2,1,0:T(8,128)(2,1)} %broadcast_select_fusion), calls=%async_computation.1 | async-start | bytes 2097152 | tf_op jit(solution)/shard_map/all_to_all | solution.py:60
  270.1 1.1 gather_fusion
  272.5 10.3 %all-to-all-done = bf16[16,128,256]{2,1,0:T(8,128)(2,1)} async-done(((bf16[16,128,256]{2,1,0:T(8,128)(2,1)}), bf16[16,128,256]{2,1,0:T(8,128)(2,1)}, u32[]{:S(2)}, u32[]{:S(2)}) %all-to-all-start) | async-done | bytes 1048608 | tf_op jit(solution)/shard_map/all_to_all | solution.py:60
  282.9 2.5 gather_fusion.23
  285.3 2.5 gather_fusion.24
  287.8 2.5 gather_fusion.25
  290.3 2.5 gather_fusion.26
  292.7 2.5 gather_fusion.12
  295.2 3.1 gather_fusion.13
  298.3 3.1 gather_fusion.14
  301.4 3.1 gather_fusion.15
  304.5 3.1 gather_fusion.16
  307.6 3.1 gather_fusion.17
  310.7 3.1 gather_fusion.18
  313.9 3.1 gather_fusion.19
  317.0 3.1 gather_fusion.20
  320.1 3.1 gather_fusion.21
  323.2 3.1 gather_fusion.22
  326.3 2.1 multiply_convert_fusion.1
  329.4 3.3 fusion.25
  332.7 1.3 convolution_bitcast_fusion
  334.9 247.9 %all-reduce.5.cloned.1.call-done = (f32[256,256]{1,0:T(8,128)}, f32[256,256]{1,0:T(8,128)}) async-done(((f32[256,256]{1,0:T(8,128)}, f32[256,256]{1,0:T(8,128)}), (f32[256,256]{1,0:T(8,128)}, f32[256,256]{1,0:T(8,128)})) %all-reduce.5.cloned.1.call-update) | async-done | bytes 524304 | tf_op jit(solution)/shard_map/psum | solution.py:104
  582.8 94.5 %all-reduce.7.cloned.1.call-done = (f32[64,256]{1,0:T(8,128)}, f32[64,256]{1,0:T(8,128)}) async-done(((f32[64,256]{1,0:T(8,128)}, f32[64,256]{1,0:T(8,128)}), (f32[64,256]{1,0:T(8,128)}, f32[64,256]{1,0:T(8,128)})) %all-reduce.7.cloned.1.call-update) | async-done | bytes 131088 | tf_op jit(solution)/shard_map/psum | solution.py:103
  677.3 1.5 copy.50
  678.7 1.5 copy.51
  680.2 1.7 copy.52
  681.9 1.7 copy.53
  (194 shorter events, 31.2 us)
Async XLA Ops:
  7.2 125.6 %copy-start = (bf16[1,1,256,256]{3,2,1,0:T(8,128)(2,1)S(1)}, bf16[1,1,256,256]{3,2,1,0:T(8,128)(2,1)}, u32[]{:S(2)}) copy-start(bf16[1,1,256,256]{3,2,1,0:T(8,128)(2,1)} %param.25) | copy-start | bytes 393220
  7.2 236.3 %reduce-scatter.2.cloned.1.call-start = ((), (), s32[]{:S(2)}) async-start(), calls=%async_computation.3 | async-start | bytes 5013504 | tf_op jit(solution)/shard_map/reduce_scatter | solution.py:49
  102.5 10.1 %copy-start.17 = (bf16[64,256]{1,0:T(8,128)(2,1)S(1)}, bf16[64,256]{1,0:T(8,128)(2,1)}, u32[]{:S(2)}) copy-start(bf16[64,256]{1,0:T(8,128)(2,1)} %param.16) | copy-start | bytes 98308
  112.7 1.3 copy-start.3
  112.7 1.6 copy-start.4
  112.7 2.0 copy-start.5
  112.7 2.3 copy-start.6
  112.7 2.7 copy-start.7
  112.7 3.0 copy-start.8
  112.7 3.3 copy-start.9
  112.7 3.7 copy-start.10
  112.8 4.0 copy-start.11
  116.7 11.3 %copy-start.18 = (bf16[64,256]{1,0:T(8,128)(2,1)S(1)}, bf16[64,256]{1,0:T(8,128)(2,1)}, u32[]{:S(2)}) copy-start(bf16[64,256]{1,0:T(8,128)(2,1)} %param.17) | copy-start | bytes 98308
  127.1 1.0 copy-start.1
  130.9 0.7 copy-start.50
  130.9 1.0 copy-start.16
  130.9 1.9 copy-start.14
  206.2 22.5 %all-to-all-start.1 = ((bf16[16,128,256]{2,1,0:T(8,128)(2,1)}), bf16[16,128,256]{2,1,0:T(8,128)(2,1)S(1)}, u32[]{:S(2)}, u32[]{:S(2)}) async-start(bf16[16,128,256]{2,1,0:T(8,128)(2,1)} %bitcast.53), calls=%async_computation.2 | async-start | bytes 2097152 | tf_op jit(solution)/shard_map/all_to_all | solution.py:90
  213.7 115.7 %all-gather.2.cloned.1.call-start = ((), (), s32[]{:S(2)}) async-start(), calls=%async_computation.4 | async-start | bytes 2506752 | tf_op jit(solution)/shard_map/all_gather | solution.py:98
  219.4 8.0 %copy-start.24 = (s32[256,1]{0,1:T(1,128)}, s32[256,1]{0,1:T(1,128)S(1)}, u32[]{:S(2)}) copy-start(s32[256,1]{0,1:T(1,128)S(1)} %get-tuple-element.51) | copy-start | bytes 3076
  219.4 8.0 %copy-start.26 = (s32[256,1]{0,1:T(1,128)}, s32[256,1]{0,1:T(1,128)S(1)}, u32[]{:S(2)}) copy-start(s32[256,1]{0,1:T(1,128)S(1)} %get-tuple-element.52) | copy-start | bytes 3076
  219.4 8.0 %copy-start.28 = (s32[256,1]{0,1:T(1,128)}, s32[256,1]{0,1:T(1,128)S(1)}, u32[]{:S(2)}) copy-start(s32[256,1]{0,1:T(1,128)S(1)} %get-tuple-element.49) | copy-start | bytes 3076
  219.4 8.0 %copy-start.30 = (s32[256,1]{0,1:T(1,128)}, s32[256,1]{0,1:T(1,128)S(1)}, u32[]{:S(2)}) copy-start(s32[256,1]{0,1:T(1,128)S(1)} %get-tuple-element.50) | copy-start | bytes 3076
  219.4 8.0 %copy-start.32 = (s32[256,1]{0,1:T(1,128)}, s32[256,1]{0,1:T(1,128)S(1)}, u32[]{:S(2)}) copy-start(s32[256,1]{0,1:T(1,128)S(1)} %get-tuple-element.47) | copy-start | bytes 3076
  219.4 8.0 %copy-start.34 = (s32[256,1]{0,1:T(1,128)}, s32[256,1]{0,1:T(1,128)S(1)}, u32[]{:S(2)}) copy-start(s32[256,1]{0,1:T(1,128)S(1)} %get-tuple-element.48) | copy-start | bytes 3076
  219.4 8.0 %copy-start.36 = (s32[256,1]{0,1:T(1,128)}, s32[256,1]{0,1:T(1,128)S(1)}, u32[]{:S(2)}) copy-start(s32[256,1]{0,1:T(1,128)S(1)} %get-tuple-element.45) | copy-start | bytes 3076
  219.4 8.0 %copy-start.38 = (s32[256,1]{0,1:T(1,128)}, s32[256,1]{0,1:T(1,128)S(1)}, u32[]{:S(2)}) copy-start(s32[256,1]{0,1:T(1,128)S(1)} %get-tuple-element.46) | copy-start | bytes 3076
  219.4 8.0 %copy-start.42 = (s32[256,1]{0,1:T(1,128)}, s32[256,1]{0,1:T(1,128)S(1)}, u32[]{:S(2)}) copy-start(s32[256,1]{0,1:T(1,128)S(1)} %get-tuple-element.42) | copy-start | bytes 3076
  228.7 1.0 copy-start.2
  240.8 4.5 copy-start.44
  240.8 5.1 copy-start.41
  240.8 5.7 copy-start.43
  240.8 6.3 copy-start.49
  240.8 6.3 copy-start.40
  240.8 6.3 copy-start.22
  240.8 6.3 copy-start.23
  240.8 6.8 copy-start.20
  240.8 6.8 copy-start.21
  240.8 7.9 %copy-start.37 = (s32[256,1]{0,1:T(1,128)S(1)}, s32[256,1]{0,1:T(1,128)}, u32[]{:S(2)}) copy-start(s32[256,1]{0,1:T(1,128)} %copy-done.36) | copy-start | bytes 3076
  240.9 7.9 %copy-start.39 = (s32[256,1]{0,1:T(1,128)S(1)}, s32[256,1]{0,1:T(1,128)}, u32[]{:S(2)}) copy-start(s32[256,1]{0,1:T(1,128)} %copy-done.38) | copy-start | bytes 3076
  240.9 8.5 %copy-start.33 = (s32[256,1]{0,1:T(1,128)S(1)}, s32[256,1]{0,1:T(1,128)}, u32[]{:S(2)}) copy-start(s32[256,1]{0,1:T(1,128)} %copy-done.32) | copy-start | bytes 3076
  240.9 8.5 %copy-start.35 = (s32[256,1]{0,1:T(1,128)S(1)}, s32[256,1]{0,1:T(1,128)}, u32[]{:S(2)}) copy-start(s32[256,1]{0,1:T(1,128)} %copy-done.34) | copy-start | bytes 3076
  240.9 9.0 %copy-start.19 = (s32[1,1,16,128]{3,2,1,0:T(8,128)S(1)}, s32[1,1,16,128]{3,2,1,0:T(8,128)}, u32[]{:S(2)}) copy-start(s32[1,1,16,128]{3,2,1,0:T(8,128)} %param.21) | copy-start | bytes 24580
  258.9 10.1 %copy-start.29 = (s32[256,1]{0,1:T(1,128)S(1)}, s32[256,1]{0,1:T(1,128)}, u32[]{:S(2)}) copy-start(s32[256,1]{0,1:T(1,128)} %copy-done.28) | copy-start | bytes 3076
  258.9 10.1 %copy-start.31 = (s32[256,1]{0,1:T(1,128)S(1)}, s32[256,1]{0,1:T(1,128)}, u32[]{:S(2)}) copy-start(s32[256,1]{0,1:T(1,128)} %copy-done.30) | copy-start | bytes 3076
  258.9 10.6 %copy-start.25 = (s32[256,1]{0,1:T(1,128)S(1)}, s32[256,1]{0,1:T(1,128)}, u32[]{:S(2)}) copy-start(s32[256,1]{0,1:T(1,128)} %copy-done.24) | copy-start | bytes 3076
  258.9 10.6 %copy-start.27 = (s32[256,1]{0,1:T(1,128)S(1)}, s32[256,1]{0,1:T(1,128)}, u32[]{:S(2)}) copy-start(s32[256,1]{0,1:T(1,128)} %copy-done.26) | copy-start | bytes 3076
  261.2 11.1 %copy-start.13 = (bf16[256,256]{1,0:T(8,128)(2,1)S(1)}, bf16[256,256]{1,0:T(8,128)(2,1)}, u32[]{:S(2)}) copy-start(bf16[256,256]{1,0:T(8,128)(2,1)} %param.18) | copy-start | bytes 393220
  261.2 21.7 %all-to-all-start = ((bf16[16,128,256]{2,1,0:T(8,128)(2,1)}), bf16[16,128,256]{2,1,0:T(8,128)(2,1)}, u32[]{:S(2)}, u32[]{:S(2)}) async-start(bf16[16,128,256]{2,1,0:T(8,128)(2,1)} %broadcast_select_fusion), calls=%async_computation.1 | async-start | bytes 2097152 | tf_op jit(solution)/shard_map/all_to_all | solution.py:60
  268.1 314.7 %all-reduce.5.cloned.1.call-start = ((), (), s32[]{:S(2)}) async-start(), calls=%async_computation.5 | async-start | bytes 1048576 | tf_op jit(solution)/shard_map/psum | solution.py:104
  313.9 12.5 %copy-start.45 = (pred[256]{0:T(512)(128)(4,1)S(1)}, pred[256]{0:T(512)(128)(4,1)}, u32[]{:S(2)}) copy-start(pred[256]{0:T(512)(128)(4,1)} %get-tuple-element.73) | copy-start | bytes 772
  313.9 12.5 %copy-start.46 = (pred[256]{0:T(512)(128)(4,1)S(1)}, pred[256]{0:T(512)(128)(4,1)}, u32[]{:S(2)}) copy-start(pred[256]{0:T(512)(128)(4,1)} %get-tuple-element.74) | copy-start | bytes 772
  313.9 12.5 %copy-start.47 = (pred[256]{0:T(512)(128)(4,1)S(1)}, pred[256]{0:T(512)(128)(4,1)}, u32[]{:S(2)}) copy-start(pred[256]{0:T(512)(128)(4,1)} %get-tuple-element.75) | copy-start | bytes 772
  313.9 12.5 %copy-start.48 = (pred[256]{0:T(512)(128)(4,1)S(1)}, pred[256]{0:T(512)(128)(4,1)}, u32[]{:S(2)}) copy-start(pred[256]{0:T(512)(128)(4,1)} %get-tuple-element.76) | copy-start | bytes 772
  329.3 347.9 %all-reduce.7.cloned.1.call-start = ((), (), s32[]{:S(2)}) async-start(), calls=%async_computation.6 | async-start | bytes 262144 | tf_op jit(solution)/shard_map/psum | solution.py:103
  329.4 3.3 copy-start.12
  332.7 1.3 copy-start.15
Sparse Core Ops, SparseCore 0:
  131.1 66.7 reduce-scatter.1
  245.4 42.2 all-gather.1
  329.5 253.2 all-reduce.4
  586.5 90.7 all-reduce.6
where the time goes:
time: 700 us; the launch traced here: 690 us
  waiting for transfers between devices  353 us (50%)
  local copies, waits for them, and re-layouts  172 us (25%)
  other arithmetic  122 us (17%)
  starting transfers between devices  14.8 us (2%)
  between operations  14.7 us (2%)
  matrix products  13.2 us (2%)
    psum x1, waiting for transfers between devices, per_device(): lax.psum((local_w2_self, local_w2_neigh), ('feat', 'dom'))  248 us
    gather x10, local copies, waits for them, and re-layouts, per_device(): jnp.take(feature_table, neigh_lists[column], axis=1).astype(jnp.float32)  101 us
    psum x1, waiting for transfers between devices, per_device(): first_self, first_mean = lax.psum((first_self, first_mean), 'dom')  94.5 us
    scatter-add x15, other arithmetic, per_device(): slot_sum = slot_sum.at[where_in[:, column]].add(d_mean)  70.3 us
    gather x17, local copies, waits for them, and re-layouts, rows_of(): return jnp.take(source_table, index_rows, axis=0)  53.6 us
    unnamed x108, local copies, waits for them, and re-layouts  15.1 us
  transfers between devices with their start and end apart: 6, of which 4 were waited for; matrix products, arithmetic and copies ran while one was open for 25% of the time, Pallas kernels for 0%

commit v1 on v0

--- a/solution.py
+++ b/solution.py
@@ -101,7 +101,7 @@
     first_self = jnp.dot(left_self, piece, preferred_element_type=jnp.float32)
     first_mean = jnp.dot(left_mean, piece, preferred_element_type=jnp.float32)
     first_self, first_mean = lax.psum((first_self, first_mean), "dom")
-    second_self, second_mean = lax.psum((local_w2_self, local_w2_neigh), ("feat", "dom"))
+    second_self, second_mean = lax.psum(lax.psum((local_w2_self, local_w2_neigh), "dom"), "feat")
     return (layer_out[None, None], first_self, first_mean, second_self, second_mean)
 
 

time: 700 us -> 566 us (0.81)
  waiting for transfers between devices: 353 us -> 218 us
    psum x1, waiting for transfers between devices: 248 us -> 111 us  [per_device(): lax.psum(lax.psum((local_w2_self, local_w2_neigh), 'dom'), 'feat')]
    unnamed x108 -> x116, local copies, waits for them, and re-layouts: 15.1 us -> 15.1 us
  transfers between devices with their start and end apart: 6 -> 6, of which waited for: 4 -> 4; matrix products, arithmetic and copies ran while one was open for 25% -> 31% of each run, Pallas kernels for 0% -> 0%
where the time goes in v1:
time: 566 us; the launch traced here: 555 us
  waiting for transfers between devices  218 us (39%)
  local copies, waits for them, and re-layouts  171 us (30%)
  other arithmetic  124 us (22%)
  starting transfers between devices  14.7 us (3%)
  between operations  14.7 us (3%)
  matrix products  13.2 us (2%)
    psum x1, waiting for transfers between devices, per_device(): lax.psum(lax.psum((local_w2_self, local_w2_neigh), 'dom'), 'feat')  111 us
    gather x10, local copies, waits for them, and re-layouts, per_device(): jnp.take(feature_table, neigh_lists[column], axis=1).astype(jnp.float32)  101 us
    psum x1, waiting for transfers between devices, per_device(): first_self, first_mean = lax.psum((first_self, first_mean), 'dom')  96.3 us
    scatter-add x15, other arithmetic, per_device(): slot_sum = slot_sum.at[where_in[:, column]].add(d_mean)  70.3 us
    gather x17, local copies, waits for them, and re-layouts, rows_of(): return jnp.take(source_table, index_rows, axis=0)  52.9 us
    unnamed x116, local copies, waits for them, and re-layouts  15.1 us
  transfers between devices with their start and end apart: 6, of which 4 were waited for; matrix products, arithmetic and copies ran while one was open for 31% of the time, Pallas kernels for 0%

profile of v1, /device:TPU:2, one launch (start us, length us, event | category | flops | bytes accessed | tf_op | source)
XLA Modules:
  0.0 555.1 jit_solution(6029919208533296953)
XLA Ops:
  7.2 1.2 slice_reduce_fusion.9
  8.7 2.8 copy.24
  11.5 10.1 %gather_fusion.2 = bf16[4608,64]{1,0:T(8,128)(2,1)} fusion(bf16[64,9216]{0,1:T(8,128)(2,1)S(1)} %bitcast.99, s32[5120]{0:T(1024)S(1)} %pad_clamp_fusion.9), kind=kCustom, calls=%fused_computation.clone | custom fusion | bytes 1198080 | tf_op jit(solution)/shard_map/jit(_take)/gather | solution.py:42
  21.6 10.1 %gather_fusion.3 = bf16[4608,64]{1,0:T(8,128)(2,1)} fusion(bf16[64,9216]{0,1:T(8,128)(2,1)S(1)} %bitcast.100, s32[5120]{0:T(1024)S(1)} %pad_clamp_fusion.8), kind=kCustom, calls=%fused_computation.2.clone | custom fusion | bytes 1198080 | tf_op jit(solution)/shard_map/jit(_take)/gather | solution.py:42
  31.7 10.1 %gather_fusion.4 = bf16[4608,64]{1,0:T(8,128)(2,1)} fusion(bf16[64,9216]{0,1:T(8,128)(2,1)S(1)} %bitcast.101, s32[5120]{0:T(1024)S(1)} %pad_clamp_fusion.7), kind=kCustom, calls=%fused_computation.3.clone | custom fusion | bytes 1198080 | tf_op jit(solution)/shard_map/jit(_take)/gather | solution.py:42
  41.8 10.1 %gather_fusion.5 = bf16[4608,64]{1,0:T(8,128)(2,1)} fusion(bf16[64,9216]{0,1:T(8,128)(2,1)S(1)} %bitcast.102, s32[5120]{0:T(1024)S(1)} %pad_clamp_fusion.6), kind=kCustom, calls=%fused_computation.4.clone | custom fusion | bytes 1198080 | tf_op jit(solution)/shard_map/jit(_take)/gather | solution.py:42
  51.9 10.1 %gather_fusion.6 = bf16[4608,64]{1,0:T(8,128)(2,1)} fusion(bf16[64,9216]{0,1:T(8,128)(2,1)S(1)} %bitcast.103, s32[5120]{0:T(1024)S(1)} %pad_clamp_fusion.5), kind=kCustom, calls=%fused_computation.5.clone | custom fusion | bytes 1198080 | tf_op jit(solution)/shard_map/jit(_take)/gather | solution.py:42
  62.1 10.1 %gather_fusion.7 = bf16[4608,64]{1,0:T(8,128)(2,1)} fusion(bf16[64,9216]{0,1:T(8,128)(2,1)S(1)} %bitcast.104, s32[5120]{0:T(1024)S(1)} %pad_clamp_fusion.4), kind=kCustom, calls=%fused_computation.6.clone | custom fusion | bytes 1198080 | tf_op jit(solution)/shard_map/jit(_take)/gather | solution.py:42
  72.2 10.1 %gather_fusion.8 = bf16[4608,64]{1,0:T(8,128)(2,1)} fusion(bf16[64,9216]{0,1:T(8,128)(2,1)S(1)} %bitcast.105, s32[5120]{0:T(1024)S(1)} %pad_clamp_fusion.3), kind=kCustom, calls=%fused_computation.7.clone | custom fusion | bytes 1198080 | tf_op jit(solution)/shard_map/jit(_take)/gather | solution.py:42
  82.3 10.1 %gather_fusion.9 = bf16[4608,64]{1,0:T(8,128)(2,1)} fusion(bf16[64,9216]{0,1:T(8,128)(2,1)S(1)} %bitcast.106, s32[5120]{0:T(1024)S(1)} %pad_clamp_fusion.2), kind=kCustom, calls=%fused_computation.8.clone | custom fusion | bytes 1198080 | tf_op jit(solution)/shard_map/jit(_take)/gather | solution.py:42
  92.4 10.1 %gather_fusion.10 = bf16[4608,64]{1,0:T(8,128)(2,1)} fusion(bf16[64,9216]{0,1:T(8,128)(2,1)S(1)} %bitcast.107, s32[5120]{0:T(1024)S(1)} %pad_clamp_fusion.1), kind=kCustom, calls=%fused_computation.9.clone | custom fusion | bytes 1198080 | tf_op jit(solution)/shard_map/jit(_take)/gather | solution.py:42
  102.6 10.1 %gather_fusion.11 = bf16[4608,64]{1,0:T(8,128)(2,1)} fusion(bf16[64,9216]{0,1:T(8,128)(2,1)S(1)} %bitcast.108, s32[5120]{0:T(1024)S(1)} %pad_clamp_fusion), kind=kCustom, calls=%fused_computation.10.clone | custom fusion | bytes 1198080 | tf_op jit(solution)/shard_map/jit(_take)/gather | solution.py:42
  116.8 10.3 %multiply_convert_fusion = bf16[64,4608]{0,1:T(8,128)(2,1)S(1)} fusion(bf16[4608,64]{1,0:T(8,128)(2,1)} %gather_fusion.11, bf16[4608,64]{1,0:T(8,128)(2,1)S(1)} %copy-done.11, bf16[4608,64]{1,0:T(8,128)(2,1)S(1)} %copy-done.10, bf16[4608,64]{1,0:T(8,128)(2,1)S(1)} %copy-done.9, bf16[4608,64]{1,0:T(8,128)(2,1)S(1)} %copy-done.8, ...), kind=kLoop, calls=%fused_computation.45 | loop fusion | flops 9142272 | bytes 6534144 | tf_op jit(solution)/shard_map/convert_element_type | solution.py:43
  128.1 2.9 convolution_add_fusion
  133.0 3.4 scatter_custom_fusion
  136.4 4.7 scatter_fusion
  141.2 5.2 scatter_fusion.1
  146.3 4.7 scatter_fusion.2
  151.1 4.8 scatter_fusion.3
  155.8 4.7 scatter_fusion.4
  160.6 4.7 scatter_fusion.5
  165.3 4.8 scatter_fusion.6
  170.1 4.8 scatter_fusion.7
  174.8 4.7 scatter_fusion.8
  179.5 4.8 scatter_fusion.9
  184.3 4.8 scatter_fusion.10
  189.1 4.9 scatter_fusion.11
  194.0 4.7 scatter_fusion.12
  198.7 4.7 scatter_fusion.13
  203.4 2.8 convert_element_type.133
  206.2 7.5 %all-to-all-start.1 = ((bf16[16,128,256]{2,1,0:T(8,128)(2,1)}), bf16[16,128,256]{2,1,0:T(8,128)(2,1)S(1)}, u32[]{:S(2)}, u32[]{:S(2)}) async-start(bf16[16,128,256]{2,1,0:T(8,128)(2,1)} %bitcast.53), calls=%async_computation.2 | async-start | bytes 2097152 | tf_op jit(solution)/shard_map/all_to_all | solution.py:90
  225.5 1.8 fusion.18
  229.7 11.0 %scatter_custom_fusion.15 = f32[288,256]{1,0:T(8,128)S(1)} fusion(s32[2048]{0:T(1024)S(1)} %bitcast.115, bf16[2048,256]{1,0:T(8,128)(2,1)} %bitcast.111, f32[]{:T(128)} %constant.47.clone.1), kind=kCustom, calls=%fused_computation.46 | custom fusion | flops 1048576 | bytes 1343492 | tf_op jit(solution)/shard_map/scatter-add | solution.py:92
  240.9 2.5 scatter_fusion.14
  243.4 1.8 fusion.12
  250.5 9.0 %gather_fusion.1 = bf16[2048,256]{1,0:T(8,128)(2,1)} fusion(bf16[288,256]{1,0:T(8,128)(2,1)S(1)} %get-tuple-element.24, s32[2048]{0:T(1024)S(1)} %broadcast_clamp_fusion), kind=kCustom, calls=%fused_computation.26 | custom fusion | bytes 2105344 | tf_op jit(solution)/shard_map/jit(_take)/gather | solution.py:8
  259.5 2.3 broadcast_select_fusion
  261.8 6.8 %all-to-all-start = ((bf16[16,128,256]{2,1,0:T(8,128)(2,1)}), bf16[16,128,256]{2,1,0:T(8,128)(2,1)}, u32[]{:S(2)}, u32[]{:S(2)}) async-start(bf16[16,128,256]{2,1,0:T(8,128)(2,1)} %broadcast_select_fusion), calls=%async_computation.1 | async-start | bytes 2097152 | tf_op jit(solution)/shard_map/all_to_all | solution.py:60
  271.2 1.3 gather_fusion
  273.5 9.9 %all-to-all-done = bf16[16,128,256]{2,1,0:T(8,128)(2,1)} async-done(((bf16[16,128,256]{2,1,0:T(8,128)(2,1)}), bf16[16,128,256]{2,1,0:T(8,128)(2,1)}, u32[]{:S(2)}, u32[]{:S(2)}) %all-to-all-start) | async-done | bytes 1048608 | tf_op jit(solution)/shard_map/all_to_all | solution.py:60
  283.4 2.5 gather_fusion.23
  285.9 2.5 gather_fusion.24
  288.4 2.5 gather_fusion.25
  290.8 2.5 gather_fusion.26
  293.3 2.3 gather_fusion.12
  295.6 2.5 gather_fusion.13
  298.1 3.1 gather_fusion.14
  301.2 3.1 gather_fusion.15
  304.3 3.1 gather_fusion.16
  307.4 3.1 gather_fusion.17
  310.5 3.1 gather_fusion.18
  313.7 3.1 gather_fusion.19
  316.8 3.1 gather_fusion.20
  319.9 3.1 gather_fusion.21
  323.0 3.1 gather_fusion.22
  326.1 2.0 multiply_convert_fusion.1
  329.1 3.3 fusion.25
  332.4 1.3 convolution_bitcast_fusion
  333.7 96.3 %all-reduce.5.cloned.1.call-done = (f32[64,256]{1,0:T(8,128)}, f32[64,256]{1,0:T(8,128)}, f32[256,256]{1,0:T(8,128)}, f32[256,256]{1,0:T(8,128)}) async-done(((f32[64,256]{1,0:T(8,128)}, f32[64,256]{1,0:T(8,128)}, f32[256,256]{1,0:T(8,128)}, f32[256,256]{1,0:T(8,128)}), (f32[64,256]{1,0:T(8,128)}, f32[64,256]{1,0:T(8,128)}, f32[256,256]{1,0:T(8,128)}, f32[256,256]{1,0:T(8,128)})) %all-reduce.5.cloned.1.call-update) | async-done | bytes 655376 | tf_op jit(solution)/shard_map/psum | solution.py:103
  431.2 110.9 %all-reduce.7.cloned.1.call-done = (f32[256,256]{1,0:T(8,128)}, f32[256,256]{1,0:T(8,128)}) async-done(((f32[256,256]{1,0:T(8,128)}, f32[256,256]{1,0:T(8,128)}), (f32[256,256]{1,0:T(8,128)}, f32[256,256]{1,0:T(8,128)})) %all-reduce.7.cloned.1.call-update) | async-done | bytes 524304 | tf_op jit(solution)/shard_map/psum | solution.py:104
  542.1 1.5 copy.52
  543.6 1.5 copy.53
  545.0 1.7 copy.54
  546.7 1.7 copy.55
  (202 shorter events, 32.4 us)
Async XLA Ops:
  7.2 125.6 %copy-start = (bf16[1,1,256,256]{3,2,1,0:T(8,128)(2,1)S(1)}, bf16[1,1,256,256]{3,2,1,0:T(8,128)(2,1)}, u32[]{:S(2)}) copy-start(bf16[1,1,256,256]{3,2,1,0:T(8,128)(2,1)} %param.25) | copy-start | bytes 393220
  7.2 236.3 %reduce-scatter.2.cloned.1.call-start = ((), (), s32[]{:S(2)}) async-start(), calls=%async_computation.3 | async-start | bytes 5013504 | tf_op jit(solution)/shard_map/reduce_scatter | solution.py:49
  102.5 10.1 %copy-start.17 = (bf16[64,256]{1,0:T(8,128)(2,1)S(1)}, bf16[64,256]{1,0:T(8,128)(2,1)}, u32[]{:S(2)}) copy-start(bf16[64,256]{1,0:T(8,128)(2,1)} %param.16) | copy-start | bytes 98308
  112.7 1.3 copy-start.3
  112.7 1.6 copy-start.4
  112.7 2.0 copy-start.5
  112.7 2.3 copy-start.6
  112.7 2.7 copy-start.7
  112.7 3.0 copy-start.8
  112.7 3.3 copy-start.9
  112.7 3.7 copy-start.10
  112.8 4.0 copy-start.11
  116.7 11.3 %copy-start.18 = (bf16[64,256]{1,0:T(8,128)(2,1)S(1)}, bf16[64,256]{1,0:T(8,128)(2,1)}, u32[]{:S(2)}) copy-start(bf16[64,256]{1,0:T(8,128)(2,1)} %param.17) | copy-start | bytes 98308
  127.1 1.0 copy-start.1
  130.9 0.7 copy-start.54
  130.9 1.0 copy-start.16
  130.9 1.9 copy-start.14
  206.2 22.5 %all-to-all-start.1 = ((bf16[16,128,256]{2,1,0:T(8,128)(2,1)}), bf16[16,128,256]{2,1,0:T(8,128)(2,1)S(1)}, u32[]{:S(2)}, u32[]{:S(2)}) async-start(bf16[16,128,256]{2,1,0:T(8,128)(2,1)} %bitcast.53), calls=%async_computation.2 | async-start | bytes 2097152 | tf_op jit(solution)/shard_map/all_to_all | solution.py:90
  213.7 115.4 %all-gather.2.cloned.1.call-start = ((), (), s32[]{:S(2)}) async-start(), calls=%async_computation.4 | async-start | bytes 2506752 | tf_op jit(solution)/shard_map/all_gather | solution.py:98
  219.4 8.0 %copy-start.24 = (s32[256,1]{0,1:T(1,128)}, s32[256,1]{0,1:T(1,128)S(1)}, u32[]{:S(2)}) copy-start(s32[256,1]{0,1:T(1,128)S(1)} %get-tuple-element.53) | copy-start | bytes 3076
  219.4 8.0 %copy-start.26 = (s32[256,1]{0,1:T(1,128)}, s32[256,1]{0,1:T(1,128)S(1)}, u32[]{:S(2)}) copy-start(s32[256,1]{0,1:T(1,128)S(1)} %get-tuple-element.54) | copy-start | bytes 3076
  219.4 8.0 %copy-start.28 = (s32[256,1]{0,1:T(1,128)}, s32[256,1]{0,1:T(1,128)S(1)}, u32[]{:S(2)}) copy-start(s32[256,1]{0,1:T(1,128)S(1)} %get-tuple-element.51) | copy-start | bytes 3076
  219.4 8.0 %copy-start.30 = (s32[256,1]{0,1:T(1,128)}, s32[256,1]{0,1:T(1,128)S(1)}, u32[]{:S(2)}) copy-start(s32[256,1]{0,1:T(1,128)S(1)} %get-tuple-element.52) | copy-start | bytes 3076
  219.4 8.0 %copy-start.32 = (s32[256,1]{0,1:T(1,128)}, s32[256,1]{0,1:T(1,128)S(1)}, u32[]{:S(2)}) copy-start(s32[256,1]{0,1:T(1,128)S(1)} %get-tuple-element.49) | copy-start | bytes 3076
  219.4 8.0 %copy-start.34 = (s32[256,1]{0,1:T(1,128)}, s32[256,1]{0,1:T(1,128)S(1)}, u32[]{:S(2)}) copy-start(s32[256,1]{0,1:T(1,128)S(1)} %get-tuple-element.50) | copy-start | bytes 3076
  219.4 8.0 %copy-start.36 = (s32[256,1]{0,1:T(1,128)}, s32[256,1]{0,1:T(1,128)S(1)}, u32[]{:S(2)}) copy-start(s32[256,1]{0,1:T(1,128)S(1)} %get-tuple-element.47) | copy-start | bytes 3076
  219.4 8.0 %copy-start.38 = (s32[256,1]{0,1:T(1,128)}, s32[256,1]{0,1:T(1,128)S(1)}, u32[]{:S(2)}) copy-start(s32[256,1]{0,1:T(1,128)S(1)} %get-tuple-element.48) | copy-start | bytes 3076
  219.4 8.0 %copy-start.42 = (s32[256,1]{0,1:T(1,128)}, s32[256,1]{0,1:T(1,128)S(1)}, u32[]{:S(2)}) copy-start(s32[256,1]{0,1:T(1,128)S(1)} %get-tuple-element.44) | copy-start | bytes 3076
  228.7 1.0 copy-start.2
  240.8 4.5 copy-start.46
  240.8 5.1 copy-start.44
  240.8 5.7 %copy-start.45 = (s32[256]{0:T(256)S(1)}, s32[256]{0:T(256)}, u32[]{:S(2)}) copy-start(s32[256]{0:T(256)} %compare_select_fusion.37) | copy-start | bytes 3076
  240.8 6.3 %copy-start.41 = (s32[256,1]{0,1:T(1,128)S(1)}, s32[256,1]{0,1:T(1,128)}, u32[]{:S(2)}) copy-start(s32[256,1]{0,1:T(1,128)} %get-tuple-element.46) | copy-start | bytes 3076
  240.8 6.9 %copy-start.43 = (s32[256,1]{0,1:T(1,128)S(1)}, s32[256,1]{0,1:T(1,128)}, u32[]{:S(2)}) copy-start(s32[256,1]{0,1:T(1,128)} %copy-done.42) | copy-start | bytes 3076
  240.8 7.4 %copy-start.53 = (s32[1,1,256]{2,1,0:T(1,128)S(1)}, s32[1,1,256]{2,1,0:T(1,128)}, u32[]{:S(2)}) copy-start(s32[1,1,256]{2,1,0:T(1,128)} %param.24) | copy-start | bytes 3076
  240.8 7.4 %copy-start.40 = (s32[256,1]{0,1:T(1,128)S(1)}, s32[256,1]{0,1:T(1,128)}, u32[]{:S(2)}) copy-start(s32[256,1]{0,1:T(1,128)} %get-tuple-element.45) | copy-start | bytes 3076
  240.8 7.4 %copy-start.22 = (s32[256,1]{0,1:T(1,128)S(1)}, s32[256,1]{0,1:T(1,128)}, u32[]{:S(2)}) copy-start(s32[256,1]{0,1:T(1,128)} %get-tuple-element.40) | copy-start | bytes 3076
  240.8 7.4 %copy-start.23 = (s32[256,1]{0,1:T(1,128)S(1)}, s32[256,1]{0,1:T(1,128)}, u32[]{:S(2)}) copy-start(s32[256,1]{0,1:T(1,128)} %get-tuple-element.41) | copy-start | bytes 3076
  240.8 8.0 %copy-start.20 = (s32[256,1]{0,1:T(1,128)S(1)}, s32[256,1]{0,1:T(1,128)}, u32[]{:S(2)}) copy-start(s32[256,1]{0,1:T(1,128)} %get-tuple-element.42) | copy-start | bytes 3076
  240.9 8.0 %copy-start.21 = (s32[256,1]{0,1:T(1,128)S(1)}, s32[256,1]{0,1:T(1,128)}, u32[]{:S(2)}) copy-start(s32[256,1]{0,1:T(1,128)} %get-tuple-element.43) | copy-start | bytes 3076
  240.9 9.1 %copy-start.37 = (s32[256,1]{0,1:T(1,128)S(1)}, s32[256,1]{0,1:T(1,128)}, u32[]{:S(2)}) copy-start(s32[256,1]{0,1:T(1,128)} %copy-done.36) | copy-start | bytes 3076
  240.9 9.1 %copy-start.39 = (s32[256,1]{0,1:T(1,128)S(1)}, s32[256,1]{0,1:T(1,128)}, u32[]{:S(2)}) copy-start(s32[256,1]{0,1:T(1,128)} %copy-done.38) | copy-start | bytes 3076
  240.9 9.6 %copy-start.19 = (s32[1,1,16,128]{3,2,1,0:T(8,128)S(1)}, s32[1,1,16,128]{3,2,1,0:T(8,128)}, u32[]{:S(2)}) copy-start(s32[1,1,16,128]{3,2,1,0:T(8,128)} %param.21) | copy-start | bytes 24580
  248.2 24.3 %copy-start.47 = (pred[256]{0:T(512)(128)(4,1)}, pred[256]{0:T(512)(128)(4,1)S(1)}, u32[]{:S(2)}) copy-start(pred[256]{0:T(512)(128)(4,1)S(1)} %compare_and_fusion.26) | copy-start | bytes 772
  259.5 10.0 %copy-start.33 = (s32[256,1]{0,1:T(1,128)S(1)}, s32[256,1]{0,1:T(1,128)}, u32[]{:S(2)}) copy-start(s32[256,1]{0,1:T(1,128)} %copy-done.32) | copy-start | bytes 3076
  259.5 10.0 %copy-start.35 = (s32[256,1]{0,1:T(1,128)S(1)}, s32[256,1]{0,1:T(1,128)}, u32[]{:S(2)}) copy-start(s32[256,1]{0,1:T(1,128)} %copy-done.34) | copy-start | bytes 3076
  259.5 10.5 %copy-start.29 = (s32[256,1]{0,1:T(1,128)S(1)}, s32[256,1]{0,1:T(1,128)}, u32[]{:S(2)}) copy-start(s32[256,1]{0,1:T(1,128)} %copy-done.28) | copy-start | bytes 3076
  259.5 10.5 %copy-start.31 = (s32[256,1]{0,1:T(1,128)S(1)}, s32[256,1]{0,1:T(1,128)}, u32[]{:S(2)}) copy-start(s32[256,1]{0,1:T(1,128)} %copy-done.30) | copy-start | bytes 3076
  259.5 11.1 %copy-start.25 = (s32[256,1]{0,1:T(1,128)S(1)}, s32[256,1]{0,1:T(1,128)}, u32[]{:S(2)}) copy-start(s32[256,1]{0,1:T(1,128)} %copy-done.24) | copy-start | bytes 3076
  259.5 11.1 %copy-start.27 = (s32[256,1]{0,1:T(1,128)S(1)}, s32[256,1]{0,1:T(1,128)}, u32[]{:S(2)}) copy-start(s32[256,1]{0,1:T(1,128)} %copy-done.26) | copy-start | bytes 3076
  261.8 21.6 %all-to-all-start = ((bf16[16,128,256]{2,1,0:T(8,128)(2,1)}), bf16[16,128,256]{2,1,0:T(8,128)(2,1)}, u32[]{:S(2)}, u32[]{:S(2)}) async-start(bf16[16,128,256]{2,1,0:T(8,128)(2,1)} %broadcast_select_fusion), calls=%async_computation.1 | async-start | bytes 2097152 | tf_op jit(solution)/shard_map/all_to_all | solution.py:60
  268.6 161.4 %all-reduce.5.cloned.1.call-start = ((), (), s32[]{:S(2)}) async-start(), calls=%async_computation.5 | async-start | bytes 1310720 | tf_op jit(solution)/shard_map/psum | solution.py:103
  313.6 12.5 %copy-start.49 = (pred[256]{0:T(512)(128)(4,1)S(1)}, pred[256]{0:T(512)(128)(4,1)}, u32[]{:S(2)}) copy-start(pred[256]{0:T(512)(128)(4,1)} %get-tuple-element.75) | copy-start | bytes 772
  313.6 12.5 %copy-start.50 = (pred[256]{0:T(512)(128)(4,1)S(1)}, pred[256]{0:T(512)(128)(4,1)}, u32[]{:S(2)}) copy-start(pred[256]{0:T(512)(128)(4,1)} %get-tuple-element.76) | copy-start | bytes 772
  313.6 12.5 %copy-start.51 = (pred[256]{0:T(512)(128)(4,1)S(1)}, pred[256]{0:T(512)(128)(4,1)}, u32[]{:S(2)}) copy-start(pred[256]{0:T(512)(128)(4,1)} %get-tuple-element.77) | copy-start | bytes 772
  313.7 12.5 %copy-start.52 = (pred[256]{0:T(512)(128)(4,1)S(1)}, pred[256]{0:T(512)(128)(4,1)}, u32[]{:S(2)}) copy-start(pred[256]{0:T(512)(128)(4,1)} %get-tuple-element.78) | copy-start | bytes 772
  329.1 3.3 copy-start.12
  332.4 97.7 %copy-start.13 = (bf16[256,256]{1,0:T(8,128)(2,1)S(1)}, bf16[256,256]{1,0:T(8,128)(2,1)}, u32[]{:S(2)}) copy-start(bf16[256,256]{1,0:T(8,128)(2,1)} %param.18) | copy-start | bytes 393220
  332.4 97.7 %copy-start.48 = (pred[256]{0:T(512)(128)(4,1)S(1)}, pred[256]{0:T(512)(128)(4,1)}, u32[]{:S(2)}) copy-start(pred[256]{0:T(512)(128)(4,1)} %copy-done.47) | copy-start | bytes 772
  332.4 98.0 %copy-start.15 = (bf16[256,256]{1,0:T(8,128)(2,1)S(1)}, bf16[256,256]{1,0:T(8,128)(2,1)}, u32[]{:S(2)}) copy-start(bf16[256,256]{1,0:T(8,128)(2,1)} %param.19) | copy-start | bytes 393220
  333.7 208.4 %all-reduce.7.cloned.1.call-start = ((), (), s32[]{:S(2)}) async-start(), calls=%async_computation.6 | async-start | bytes 1048576 | tf_op jit(solution)/shard_map/psum | solution.py:104
Sparse Core Ops, SparseCore 0:
  131.1 66.7 reduce-scatter.1
  245.4 42.1 all-gather.1
  333.8 96.2 all-reduce.4
  432.3 109.7 all-reduce.6
